TPU v7x, 256 devices: a whole 4x4x8 slice. The times are simulated.
256 devices in a mesh: expert: 2 (over z_lo), batch: 4 (over x), seq: 32 (over y, z_hi, core).
Axes of the slice: x: 4, y: 4, z: 8 (z_hi: 4, z_lo: 2; z = z_hi * 2 + z_lo), core: 2. Of those that a mesh axis runs over, the one named last changes fastest.
Arguments:
- queries: bfloat16 [2, 4, 2, 3072, 4096], P('expert', 'batch', None, 'seq'), may hold values from -36 to 36
- keys: bfloat16 [2, 4, 2, 3072, 4096], P('expert', 'batch', None, 'seq'), may hold values from -21 to 21
- values: bfloat16 [2, 4, 2, 3072, 4096], P('expert', 'batch', None, 'seq'), may hold values from -6 to 6
- latents: bfloat16 [2, 4, 3072, 4096], P('expert', 'batch', 'seq'), may hold values from -6 to 6
- gain: bfloat16 [2, 4096], P('expert'), may hold values from 0.099609375 to 1.8984375
- steps_table: int32 [2, 4], P('expert', 'batch'), may hold values from 0 to 38
- flags: int32 [4], P('batch'), may hold values 0 or 1
Outputs:
- denoised: bfloat16 [2, 4, 3072, 4096], P('expert', 'batch', 'seq')
- next_latents: bfloat16 [2, 4, 3072, 4096], P('expert', 'batch', 'seq')
All inputs are finite; a program needn't handle non-finite values. No bound on the sum of `flags` on one device may be relied on, other than what follows from the above.
Results may differ from a plain program's by a relative error of at most 0.006.
Values may be sent and summed in bfloat16 or wider, within the bound.
No kernel may reach another device: no remote copies, remote signals or barrier semaphores. Data moves between devices by JAX's collectives and lax.ppermute only.
A program may use at most 64 MiB of HBM per device.

v0:
```python
import jax
import jax.numpy as jnp
from jax import lax
from jax.sharding import Mesh
from jax.sharding import PartitionSpec as P

HDIM = 128
STEPS = 40
SEQ = ("seq_0", "seq_1", "seq_2")
GUIDANCE = 3.5
flow_shift = 5.0


def split_up(value, dim, peers):
    lengths = value.shape
    tiles = value.reshape(*lengths[:dim], peers, lengths[dim] // peers, *lengths[dim + 1 :])
    return jnp.moveaxis(tiles, dim, 0)


def joined_along(tiles, dim):
    tiles = jnp.moveaxis(tiles, 0, dim)
    lengths = tiles.shape
    return tiles.reshape(*lengths[:dim], lengths[dim] * lengths[dim + 1], *lengths[dim + 2 :])


def exchange_in_order(tiles, axes, sequence):
    inside = tiles.shape[1:]
    out = tiles.reshape(*(lax.axis_size(a) for a in axes), *inside)
    for k in sequence:
        out = lax.all_to_all(out, axes[k], k, k, tiled=True)
    return out.reshape(-1, *inside)


def exchange_by_chip(value, groups, sequence, split_dim, concat_dim):
    peers = lax.axis_size(groups[0]) * lax.axis_size(groups[1])
    tiles = split_up(value, split_dim, peers)
    return joined_along(exchange_in_order(tiles, groups, sequence), concat_dim)


def from_partner(block, axis, bit):
    count = lax.axis_size(axis)
    route = []
    for low in range(count):
        high = low | 1 << bit
        if high != low and high < count:
            route += [(low, high), (high, low)]
    return lax.ppermute(block, axis, route)


def sigma_of(step):
    level = 1.0 - step.astype(jnp.float32) / STEPS
    return flow_shift * level / (1.0 + (flow_shift - 1.0) * level)


def combine(cond, uncond):
    base = uncond.astype(jnp.float32)
    return (base + GUIDANCE * (cond.astype(jnp.float32) - base)).astype(jnp.bfloat16)


def attend(stacked):
    query_heads, key_heads, value_heads = stacked
    items, length, width_dev = query_heads.shape
    heads_dev = width_dev // HDIM
    block = 512
    key_rows = key_heads.reshape(items, length, heads_dev, HDIM)
    value_rows = value_heads.reshape(items, length, heads_dev, HDIM)
    query_blocks = query_heads.reshape(items, length // block, block, heads_dev, HDIM).transpose(
        1, 0, 2, 3, 4
    )

    def one_block(query_part):
        scores = jnp.einsum(
            "nqhd,nkhd->nhqk", query_part, key_rows, preferred_element_type=jnp.float32
        ) * HDIM ** (-0.5)
        weights = jax.nn.softmax(scores, axis=-1).astype(jnp.bfloat16)
        return jnp.einsum(
            "nhqk,nkhd->nqhd", weights, value_rows, preferred_element_type=jnp.float32
        ).astype(jnp.bfloat16)

    result = lax.map(one_block, query_blocks)
    return result.transpose(1, 0, 2, 3, 4).reshape(items, length, width_dev)


def per_device(queries, keys, values, latents, gain, steps_table, flags):
    attended = attend(
        (
            exchange_by_chip(queries[0, 0], (("seq_0", "seq_1"), "seq_2"), (0, 1), 2, 1),
            exchange_by_chip(keys[0, 0], (("seq_0", "seq_1"), "seq_2"), (0, 1), 2, 1),
            exchange_by_chip(values[0, 0], (("seq_0", "seq_1"), "seq_2"), (0, 1), 2, 1),
        )
    )
    guided = lax.all_to_all(
        combine(attended[0], attended[1]), SEQ, split_axis=0, concat_axis=1, tiled=True
    )
    guided_f32 = guided.astype(jnp.float32)
    scale = lax.rsqrt(jnp.mean(guided_f32 * guided_f32, axis=-1, keepdims=True) + 1e-06)
    velocity = guided_f32 * scale * gain[0].astype(jnp.float32)[None, :]
    step_now = steps_table[0, 0]
    sigma_now = sigma_of(step_now)
    sigma_next = sigma_of(step_now + 1)
    current = latents[0, 0].astype(jnp.float32)
    denoised = (current - sigma_now * velocity).astype(jnp.bfloat16)
    moved = (current + (sigma_next - sigma_now) * velocity).astype(jnp.bfloat16)
    partner = from_partner(moved, "expert", 0)
    next_latents = jnp.where(flags[0] == 1, partner, moved)
    return (denoised[None, None], next_latents[None, None])


def solution(mesh):
    torus = Mesh(
        mesh.devices.reshape(mesh.shape["expert"], mesh.shape["batch"], 4, 4, 2),
        ("expert", "batch", "seq_0", "seq_1", "seq_2"),
    )
    placed = (
        P("expert", "batch", None, SEQ, None),
        P("expert", "batch", None, SEQ, None),
        P("expert", "batch", None, SEQ, None),
        P("expert", "batch", SEQ, None),
        P("expert", None),
        P("expert", "batch"),
        P("batch"),
    )
    return jax.shard_map(
        per_device,
        mesh=torus,
        in_specs=placed,
        out_specs=(P("expert", "batch", SEQ, None), P("expert", "batch", SEQ, None)),
        check_vma=False,
    )
```

profile of v0, /device:TPU:6, one launch (start us, length us, event | category | flops | bytes accessed | tf_op | source)
XLA Modules:
  0.0 393.9 jit_solution(4078479257126038862)
XLA Ops:
  0.6 1.7 copy.64
  2.4 1.8 copy.43
  4.1 0.0 copy-start.1
  4.1 11.3 %all-to-all-start.2 = ((bf16[16,2,2,96,128]{4,3,1,2,0:T(8,128)(2,1)}), bf16[16,2,2,96,128]{4,3,1,2,0:T(8,128)(2,1)S(1)}, u32[]{:S(2)}, u32[]{:S(2)}) async-start(bf16[16,2,2,96,128]{4,3,1,2,0:T(8,128)(2,1)} %copy.43), calls=%async_computation.2 | async-start | bytes 3145728 | tf_op jit(solution)/shard_map/all_to_all | solution.py:30
  15.5 0.0 copy-done.1
  15.5 0.3 copy.65
  15.8 1.8 copy.48
  17.6 39.5 %all-to-all-done.2 = bf16[16,2,2,96,128]{4,3,1,2,0:T(8,128)(2,1)S(1)} async-done(((bf16[16,2,2,96,128]{4,3,1,2,0:T(8,128)(2,1)}), bf16[16,2,2,96,128]{4,3,1,2,0:T(8,128)(2,1)S(1)}, u32[]{:S(2)}, u32[]{:S(2)}) %all-to-all-start.2) | async-done | bytes 1572896 | tf_op jit(solution)/shard_map/all_to_all | solution.py:30
  57.1 0.1 copy.44
  57.2 5.0 %all_to_all.40 = bf16[16,2,2,96,128]{4,3,0,2,1:T(8,128)(2,1)S(1)} all-to-all(bf16[16,2,2,96,128]{4,3,0,2,1:T(8,128)(2,1)S(1)} %copy.44), channel_id=1, replica_groups=mesh['expert'=2,'batch'=4,'seq_0'=4,'seq_1'=4,'seq_2'=2] {'seq_2'}, dimensions={1} | all-to-all | bytes 3145728 | tf_op jit(solution)/shard_map/all_to_all | solution.py:30
  62.2 3.7 all-to-all-start.4
  66.0 1.7 copy.63
  67.7 1.8 copy.39
  69.5 37.3 %all-to-all-done.4 = bf16[16,2,2,96,128]{4,3,1,2,0:T(8,128)(2,1)S(1)} async-done(((bf16[16,2,2,96,128]{4,3,1,2,0:T(8,128)(2,1)}), bf16[16,2,2,96,128]{4,3,1,2,0:T(8,128)(2,1)S(1)}, u32[]{:S(2)}, u32[]{:S(2)}) %all-to-all-start.4) | async-done | bytes 1572896 | tf_op jit(solution)/shard_map/all_to_all | solution.py:30
  106.8 5.2 %all-to-all-start = ((bf16[16,2,2,96,128]{4,3,1,2,0:T(8,128)(2,1)}), bf16[16,2,2,96,128]{4,3,1,2,0:T(8,128)(2,1)}, u32[]{:S(2)}, u32[]{:S(2)}) async-start(bf16[16,2,2,96,128]{4,3,1,2,0:T(8,128)(2,1)} %copy.39), calls=%async_computation | async-start | bytes 3145728 | tf_op jit(solution)/shard_map/all_to_all | solution.py:30
  112.0 0.2 copy.45
  112.2 0.1 copy.46
  112.3 1.3 copy.49
  113.6 36.0 %all-to-all-done = bf16[16,2,2,96,128]{4,3,1,2,0:T(8,128)(2,1)} async-done(((bf16[16,2,2,96,128]{4,3,1,2,0:T(8,128)(2,1)}), bf16[16,2,2,96,128]{4,3,1,2,0:T(8,128)(2,1)}, u32[]{:S(2)}, u32[]{:S(2)}) %all-to-all-start) | async-done | bytes 1572896 | tf_op jit(solution)/shard_map/all_to_all | solution.py:30
  149.6 3.7 all-to-all-start.5
  153.2 2.7 copy.40
  155.9 0.0 all-to-all-done.5
  155.9 4.8 %all-to-all-start.1 = ((bf16[16,2,2,96,128]{4,3,0,2,1:T(8,128)(2,1)}), bf16[16,2,2,96,128]{4,3,0,2,1:T(8,128)(2,1)}, u32[]{:S(2)}, u32[]{:S(2)}) async-start(bf16[16,2,2,96,128]{4,3,0,2,1:T(8,128)(2,1)} %copy.40), calls=%async_computation.1 | async-start | bytes 3145728 | tf_op jit(solution)/shard_map/all_to_all | solution.py:30
  160.7 0.2 copy.50
  160.9 1.3 copy.51
  162.2 1.1 all-to-all-done.1
  163.4 1.6 copy.41
  165.0 173.4 %while.10 = (s32[]{:T(128)}, bf16[6,2,512,1,128]{4,2,1,3,0:T(8,128)(2,1)}, bf16[6,2,512,1,128]{4,2,0,1,3:T(8,128)(2,1)S(1)}, bf16[2,3072,1,128]{3,1,0,2:T(8,128)...) while((s32[]{:T(128)}, bf16[6,2,512,1,128]{4,2,1,3,0:T(8,128)(2,1)}, ...), condition=%wide.region_3.4_spmd, body=%wide.region_0.3_spmd.sunk | while | flops 1639062528 | bytes 54009940 | solution.py:80
  165.0 6.3 %fusion.50 = f32[2,512,3072]{2,1,0:T(8,128)} fusion(bf16[2,3072,1,128]{3,1,0,2:T(8,128)(2,1)S(1)} %get-tuple-element.110, bf16[6,2,512,1,128]{4,2,0,1,3:T(8,128)(2,1)S(1)} %get-tuple-element.109, s32[]{:T(128)S(6)} %copy.70), kind=kOutput, calls=%fused_computation.8.clone.1 | convolution fusion | flops 805306368 | bytes 14417924 | tf_op jit(solution)/shard_map/while/body/eval_jaxpr/nqhd,nkhd->nhqk/dot_general | solution.py:72
  171.3 11.2 %fusion.51 = f32[2,512]{1,0:T(2,128)S(1)} fusion(f32[2,512,3072]{2,1,0:T(8,128)} %fusion.50), kind=kOutput, calls=%fused_computation.37.clone.1 | output fusion | flops 12585983 | bytes 12587008 | tf_op jit(solution)/shard_map/while/body/eval_jaxpr/sub | solution.py:75
  182.5 11.4 %fusion.52 = bf16[6,2,512,1,128]{4,2,1,3,0:T(8,128)(2,1)} fusion(bf16[6,2,512,1,128]{4,2,1,3,0:T(8,128)(2,1)} %get-tuple-element.102, s32[]{:T(128)S(6)} %copy.70, bf16[2,3072,1,128]{3,1,0,2:T(8,128)(2,1)} %get-tuple-element.111, f32[2,512]{1,0:T(2,128)S(1)} %fusion.51, f32[2,512,3072]{2,1,0:T(8,128)} %fusion.50), kind=kOutput, calls=%fused_computation.12.clone.1 | convolution fusion | flops 821170176 | bytes 27004932 | tf_op jit(solution)/shard_map/while/body/eval_jaxpr/nhqk,nkhd->nqhd/dot_general | solution.py:76
  193.9 6.3 %fusion.50 = f32[2,512,3072]{2,1,0:T(8,128)} fusion(bf16[2,3072,1,128]{3,1,0,2:T(8,128)(2,1)S(1)} %get-tuple-element.110, bf16[6,2,512,1,128]{4,2,0,1,3:T(8,128)(2,1)S(1)} %get-tuple-element.109, s32[]{:T(128)S(6)} %copy.70), kind=kOutput, calls=%fused_computation.8.clone.1 | convolution fusion | flops 805306368 | bytes 14417924 | tf_op jit(solution)/shard_map/while/body/eval_jaxpr/nqhd,nkhd->nhqk/dot_general | solution.py:72
  200.2 11.2 %fusion.51 = f32[2,512]{1,0:T(2,128)S(1)} fusion(f32[2,512,3072]{2,1,0:T(8,128)} %fusion.50), kind=kOutput, calls=%fused_computation.37.clone.1 | output fusion | flops 12585983 | bytes 12587008 | tf_op jit(solution)/shard_map/while/body/eval_jaxpr/sub | solution.py:75
  211.4 11.4 %fusion.52 = bf16[6,2,512,1,128]{4,2,1,3,0:T(8,128)(2,1)} fusion(bf16[6,2,512,1,128]{4,2,1,3,0:T(8,128)(2,1)} %get-tuple-element.102, s32[]{:T(128)S(6)} %copy.70, bf16[2,3072,1,128]{3,1,0,2:T(8,128)(2,1)} %get-tuple-element.111, f32[2,512]{1,0:T(2,128)S(1)} %fusion.51, f32[2,512,3072]{2,1,0:T(8,128)} %fusion.50), kind=kOutput, calls=%fused_computation.12.clone.1 | convolution fusion | flops 821170176 | bytes 27004932 | tf_op jit(solution)/shard_map/while/body/eval_jaxpr/nhqk,nkhd->nqhd/dot_general | solution.py:76
  222.8 6.3 %fusion.50 = f32[2,512,3072]{2,1,0:T(8,128)} fusion(bf16[2,3072,1,128]{3,1,0,2:T(8,128)(2,1)S(1)} %get-tuple-element.110, bf16[6,2,512,1,128]{4,2,0,1,3:T(8,128)(2,1)S(1)} %get-tuple-element.109, s32[]{:T(128)S(6)} %copy.70), kind=kOutput, calls=%fused_computation.8.clone.1 | convolution fusion | flops 805306368 | bytes 14417924 | tf_op jit(solution)/shard_map/while/body/eval_jaxpr/nqhd,nkhd->nhqk/dot_general | solution.py:72
  229.1 11.2 %fusion.51 = f32[2,512]{1,0:T(2,128)S(1)} fusion(f32[2,512,3072]{2,1,0:T(8,128)} %fusion.50), kind=kOutput, calls=%fused_computation.37.clone.1 | output fusion | flops 12585983 | bytes 12587008 | tf_op jit(solution)/shard_map/while/body/eval_jaxpr/sub | solution.py:75
  240.3 11.4 %fusion.52 = bf16[6,2,512,1,128]{4,2,1,3,0:T(8,128)(2,1)} fusion(bf16[6,2,512,1,128]{4,2,1,3,0:T(8,128)(2,1)} %get-tuple-element.102, s32[]{:T(128)S(6)} %copy.70, bf16[2,3072,1,128]{3,1,0,2:T(8,128)(2,1)} %get-tuple-element.111, f32[2,512]{1,0:T(2,128)S(1)} %fusion.51, f32[2,512,3072]{2,1,0:T(8,128)} %fusion.50), kind=kOutput, calls=%fused_computation.12.clone.1 | convolution fusion | flops 821170176 | bytes 27004932 | tf_op jit(solution)/shard_map/while/body/eval_jaxpr/nhqk,nkhd->nqhd/dot_general | solution.py:76
  251.7 6.3 %fusion.50 = f32[2,512,3072]{2,1,0:T(8,128)} fusion(bf16[2,3072,1,128]{3,1,0,2:T(8,128)(2,1)S(1)} %get-tuple-element.110, bf16[6,2,512,1,128]{4,2,0,1,3:T(8,128)(2,1)S(1)} %get-tuple-element.109, s32[]{:T(128)S(6)} %copy.70), kind=kOutput, calls=%fused_computation.8.clone.1 | convolution fusion | flops 805306368 | bytes 14417924 | tf_op jit(solution)/shard_map/while/body/eval_jaxpr/nqhd,nkhd->nhqk/dot_general | solution.py:72
  258.0 11.2 %fusion.51 = f32[2,512]{1,0:T(2,128)S(1)} fusion(f32[2,512,3072]{2,1,0:T(8,128)} %fusion.50), kind=kOutput, calls=%fused_computation.37.clone.1 | output fusion | flops 12585983 | bytes 12587008 | tf_op jit(solution)/shard_map/while/body/eval_jaxpr/sub | solution.py:75
  269.2 11.4 %fusion.52 = bf16[6,2,512,1,128]{4,2,1,3,0:T(8,128)(2,1)} fusion(bf16[6,2,512,1,128]{4,2,1,3,0:T(8,128)(2,1)} %get-tuple-element.102, s32[]{:T(128)S(6)} %copy.70, bf16[2,3072,1,128]{3,1,0,2:T(8,128)(2,1)} %get-tuple-element.111, f32[2,512]{1,0:T(2,128)S(1)} %fusion.51, f32[2,512,3072]{2,1,0:T(8,128)} %fusion.50), kind=kOutput, calls=%fused_computation.12.clone.1 | convolution fusion | flops 821170176 | bytes 27004932 | tf_op jit(solution)/shard_map/while/body/eval_jaxpr/nhqk,nkhd->nqhd/dot_general | solution.py:76
  280.6 6.3 %fusion.50 = f32[2,512,3072]{2,1,0:T(8,128)} fusion(bf16[2,3072,1,128]{3,1,0,2:T(8,128)(2,1)S(1)} %get-tuple-element.110, bf16[6,2,512,1,128]{4,2,0,1,3:T(8,128)(2,1)S(1)} %get-tuple-element.109, s32[]{:T(128)S(6)} %copy.70), kind=kOutput, calls=%fused_computation.8.clone.1 | convolution fusion | flops 805306368 | bytes 14417924 | tf_op jit(solution)/shard_map/while/body/eval_jaxpr/nqhd,nkhd->nhqk/dot_general | solution.py:72
  286.9 11.2 %fusion.51 = f32[2,512]{1,0:T(2,128)S(1)} fusion(f32[2,512,3072]{2,1,0:T(8,128)} %fusion.50), kind=kOutput, calls=%fused_computation.37.clone.1 | output fusion | flops 12585983 | bytes 12587008 | tf_op jit(solution)/shard_map/while/body/eval_jaxpr/sub | solution.py:75
  298.1 11.4 %fusion.52 = bf16[6,2,512,1,128]{4,2,1,3,0:T(8,128)(2,1)} fusion(bf16[6,2,512,1,128]{4,2,1,3,0:T(8,128)(2,1)} %get-tuple-element.102, s32[]{:T(128)S(6)} %copy.70, bf16[2,3072,1,128]{3,1,0,2:T(8,128)(2,1)} %get-tuple-element.111, f32[2,512]{1,0:T(2,128)S(1)} %fusion.51, f32[2,512,3072]{2,1,0:T(8,128)} %fusion.50), kind=kOutput, calls=%fused_computation.12.clone.1 | convolution fusion | flops 821170176 | bytes 27004932 | tf_op jit(solution)/shard_map/while/body/eval_jaxpr/nhqk,nkhd->nqhd/dot_general | solution.py:76
  309.5 6.3 %fusion.50 = f32[2,512,3072]{2,1,0:T(8,128)} fusion(bf16[2,3072,1,128]{3,1,0,2:T(8,128)(2,1)S(1)} %get-tuple-element.110, bf16[6,2,512,1,128]{4,2,0,1,3:T(8,128)(2,1)S(1)} %get-tuple-element.109, s32[]{:T(128)S(6)} %copy.70), kind=kOutput, calls=%fused_computation.8.clone.1 | convolution fusion | flops 805306368 | bytes 14417924 | tf_op jit(solution)/shard_map/while/body/eval_jaxpr/nqhd,nkhd->nhqk/dot_general | solution.py:72
  315.8 11.2 %fusion.51 = f32[2,512]{1,0:T(2,128)S(1)} fusion(f32[2,512,3072]{2,1,0:T(8,128)} %fusion.50), kind=kOutput, calls=%fused_computation.37.clone.1 | output fusion | flops 12585983 | bytes 12587008 | tf_op jit(solution)/shard_map/while/body/eval_jaxpr/sub | solution.py:75
  327.0 11.4 %fusion.52 = bf16[6,2,512,1,128]{4,2,1,3,0:T(8,128)(2,1)} fusion(bf16[6,2,512,1,128]{4,2,1,3,0:T(8,128)(2,1)} %get-tuple-element.102, s32[]{:T(128)S(6)} %copy.70, bf16[2,3072,1,128]{3,1,0,2:T(8,128)(2,1)} %get-tuple-element.111, f32[2,512]{1,0:T(2,128)S(1)} %fusion.51, f32[2,512,3072]{2,1,0:T(8,128)} %fusion.50), kind=kOutput, calls=%fused_computation.12.clone.1 | convolution fusion | flops 821170176 | bytes 27004932 | tf_op jit(solution)/shard_map/while/body/eval_jaxpr/nhqk,nkhd->nqhd/dot_general | solution.py:76
  338.4 1.5 fusion.38
  339.9 0.0 copy-start.2
  339.9 1.2 fusion.33
  341.1 4.9 %all-to-all-start.6 = ((bf16[32,96,128]{2,1,0:T(8,128)(2,1)}), bf16[32,96,128]{2,1,0:T(8,128)(2,1)S(1)}, u32[]{:S(2)}, u32[]{:S(2)}) async-start(bf16[32,96,128]{2,1,0:T(8,128)(2,1)} %fusion.33), calls=%async_computation.6 | async-start | bytes 1572864 | tf_op jit(solution)/shard_map/all_to_all | solution.py:92
  346.6 0.0 copy-done.2
  347.4 20.1 %all-to-all-done.6 = bf16[32,96,128]{2,1,0:T(8,128)(2,1)S(1)} async-done(((bf16[32,96,128]{2,1,0:T(8,128)(2,1)}), bf16[32,96,128]{2,1,0:T(8,128)(2,1)S(1)}, u32[]{:S(2)}, u32[]{:S(2)}) %all-to-all-start.6) | async-done | bytes 786464 | tf_op jit(solution)/shard_map/all_to_all | solution.py:92
  367.5 1.4 convert_bitcast_fusion
  368.9 2.1 copy.53
  370.9 0.0 copy-start
  370.9 1.6 reshape.171
  372.6 0.3 fusion.34
  372.8 0.0 copy-done
  372.8 1.8 fusion.31
  374.6 0.1 collective-permute-start
  374.7 1.2 fusion.29
  375.9 17.0 %collective-permute-done = bf16[96,4096]{1,0:T(8,128)(2,1)S(1)} collective-permute-done((bf16[96,4096]{1,0:T(8,128)(2,1)S(1)}, bf16[96,4096]{1,0:T(8,128)(2,1)S(1)}, u32[]{:S(2)}, u32[]{:S(2)}) %collective-permute-start) | collective-permute-done | bytes 786464 | tf_op jit(solution)/shard_map/ppermute | solution.py:47
  393.0 1.0 select_bitcast_fusion
  (3 shorter events, 0.0 us)
Async XLA Ops:
  4.1 11.3 %copy-start.1 = (bf16[1,1,2,96,4096]{4,3,2,1,0:T(8,128)(2,1)S(1)}, bf16[1,1,2,96,4096]{4,3,2,1,0:T(8,128)(2,1)}, u32[]{:S(2)}) copy-start(bf16[1,1,2,96,4096]{4,3,2,1,0:T(8,128)(2,1)} %param.11) | copy-start | bytes 4718596
  4.1 53.0 %all-to-all-start.2 = ((bf16[16,2,2,96,128]{4,3,1,2,0:T(8,128)(2,1)}), bf16[16,2,2,96,128]{4,3,1,2,0:T(8,128)(2,1)S(1)}, u32[]{:S(2)}, u32[]{:S(2)}) async-start(bf16[16,2,2,96,128]{4,3,1,2,0:T(8,128)(2,1)} %copy.43), calls=%async_computation.2 | async-start | bytes 3145728 | tf_op jit(solution)/shard_map/all_to_all | solution.py:30
  62.2 44.5 %all-to-all-start.4 = ((bf16[16,2,2,96,128]{4,3,1,2,0:T(8,128)(2,1)}), bf16[16,2,2,96,128]{4,3,1,2,0:T(8,128)(2,1)S(1)}, u32[]{:S(2)}, u32[]{:S(2)}) async-start(bf16[16,2,2,96,128]{4,3,1,2,0:T(8,128)(2,1)} %copy.48), calls=%async_computation.4 | async-start | bytes 3145728 | tf_op jit(solution)/shard_map/all_to_all | solution.py:30
  106.8 42.8 %all-to-all-start = ((bf16[16,2,2,96,128]{4,3,1,2,0:T(8,128)(2,1)}), bf16[16,2,2,96,128]{4,3,1,2,0:T(8,128)(2,1)}, u32[]{:S(2)}, u32[]{:S(2)}) async-start(bf16[16,2,2,96,128]{4,3,1,2,0:T(8,128)(2,1)} %copy.39), calls=%async_computation | async-start | bytes 3145728 | tf_op jit(solution)/shard_map/all_to_all | solution.py:30
  149.6 6.4 %all-to-all-start.5 = ((bf16[16,2,2,96,128]{4,3,0,2,1:T(8,128)(2,1)}), bf16[16,2,2,96,128]{4,3,0,2,1:T(8,128)(2,1)S(1)}, u32[]{:S(2)}, u32[]{:S(2)}) async-start(bf16[16,2,2,96,128]{4,3,0,2,1:T(8,128)(2,1)} %copy.49), calls=%async_computation.5 | async-start | bytes 3145728 | tf_op jit(solution)/shard_map/all_to_all | solution.py:30
  155.9 7.4 %all-to-all-start.1 = ((bf16[16,2,2,96,128]{4,3,0,2,1:T(8,128)(2,1)}), bf16[16,2,2,96,128]{4,3,0,2,1:T(8,128)(2,1)}, u32[]{:S(2)}, u32[]{:S(2)}) async-start(bf16[16,2,2,96,128]{4,3,0,2,1:T(8,128)(2,1)} %copy.40), calls=%async_computation.1 | async-start | bytes 3145728 | tf_op jit(solution)/shard_map/all_to_all | solution.py:30
  339.9 6.8 %copy-start.2 = (bf16[1,4096]{1,0:T(2,128)(2,1)S(1)}, bf16[1,4096]{1,0:T(2,128)(2,1)}, u32[]{:S(2)}) copy-start(bf16[1,4096]{1,0:T(2,128)(2,1)} %param.13) | copy-start | bytes 24580
  341.1 26.4 %all-to-all-start.6 = ((bf16[32,96,128]{2,1,0:T(8,128)(2,1)}), bf16[32,96,128]{2,1,0:T(8,128)(2,1)S(1)}, u32[]{:S(2)}, u32[]{:S(2)}) async-start(bf16[32,96,128]{2,1,0:T(8,128)(2,1)} %fusion.33), calls=%async_computation.6 | async-start | bytes 1572864 | tf_op jit(solution)/shard_map/all_to_all | solution.py:92
  370.9 1.9 copy-start
  374.6 18.4 %collective-permute-start = (bf16[96,4096]{1,0:T(8,128)(2,1)S(1)}, bf16[96,4096]{1,0:T(8,128)(2,1)S(1)}, u32[]{:S(2)}, u32[]{:S(2)}) collective-permute-start(bf16[96,4096]{1,0:T(8,128)(2,1)S(1)} %fusion.31), channel_id=1, source_target_pairs={{0,128},{128,0},{1,129},{129,1},{2,130},{130,2},{3,131},{131,3},{4... | collective-permute-start | bytes 2359304 | tf_op jit(solution)/shard_map/ppermute | solution.py:47
where the time goes:
time: 395 us; the launch traced here: 394 us
  waiting for transfers between devices  151 us (38%)
  matrix products  106 us (27%)
  other arithmetic  73.9 us (19%)
  starting transfers between devices  33.7 us (9%)
  local copies, waits for them, and re-layouts  21.8 us (6%)
  blocking collectives  5 us (1%)
    all_to_all x5, waiting for transfers between devices, exchange_in_order(): out = lax.all_to_all(out, axes[k], k, k, tiled=True)  114 us
    dot_general x6, matrix products, one_block(): jnp.einsum('nhqk,nkhd->nqhd', weights, value_rows, preferred_element_type...  68.3 us
    sub x6, other arithmetic, one_block(): weights = jax.nn.softmax(scores, axis=-1).astype(jnp.bfloat16)  67.1 us
    dot_general x6, matrix products, one_block(): jnp.einsum('nqhd,nkhd->nhqk', query_part, key_rows, preferred_element_typ...  38 us
    all_to_all x5, starting transfers between devices, exchange_in_order(): out = lax.all_to_all(out, axes[k], k, k, tiled=True)  28.7 us
    all_to_all x1, waiting for transfers between devices, per_device(): lax.all_to_all(combine(attended[0], attended[1]), SEQ, split_axis=0, conc...  20.1 us
    ppermute x1, waiting for transfers between devices, from_partner(): return lax.ppermute(block, axis, route)  17 us
  transfers between devices with their start and end apart: 7, of which 6 were waited for; matrix products, arithmetic and copies ran while one was open for 3% of the time, Pallas kernels for 0%

commit v1 on v0

--- a/solution.py
+++ b/solution.py
@@ -89,9 +89,16 @@
             exchange_by_chip(values[0, 0], (("seq_0", "seq_1"), "seq_2"), (0, 1), 2, 1),
         )
     )
-    guided = lax.all_to_all(
-        combine(attended[0], attended[1]), SEQ, split_axis=0, concat_axis=1, tiled=True
-    )
+
+    def produce_patches(u, chip_axis):
+        return jnp.concatenate(
+            jax.lax.all_to_all(
+                jnp.stack(jnp.split(u, jax.lax.axis_size(chip_axis), axis=0)), chip_axis, 0, 0
+            ),
+            axis=1,
+        )
+
+    guided = produce_patches(combine(attended[0], attended[1]), SEQ)
     guided_f32 = guided.astype(jnp.float32)
     scale = lax.rsqrt(jnp.mean(guided_f32 * guided_f32, axis=-1, keepdims=True) + 1e-06)
     velocity = guided_f32 * scale * gain[0].astype(jnp.float32)[None, :]

time: 395 us -> 415 us (1.051)
  local copies, waits for them, and re-layouts: 21.8 us -> 38 us
  blocking collectives: 5 us -> 12.8 us
  starting transfers between devices: 33.7 us -> 28.1 us
    unnamed x9 -> x42, local copies, waits for them, and re-layouts: 3.83 us -> 24.8 us
    all_to_all x1 -> x2, blocking collectives: 5 us -> 12.8 us  [exchange_in_order(): out = lax.all_to_all(out, axes[k], k, k, tiled=True)]
    all_to_all x5 -> x4, starting transfers between devices: 28.7 us -> 22.4 us  [exchange_in_order(): out = lax.all_to_all(out, axes[k], k, k, tiled=True)]
    all_to_all x5 -> x4, waiting for transfers between devices: 114 us -> 114 us  [exchange_in_order(): out = lax.all_to_all(out, axes[k], k, k, tiled=True)]
  transfers between devices with their start and end apart: 7 -> 6, of which waited for: 6 -> 6; matrix products, arithmetic and copies ran while one was open for 3% -> 3% of each run, Pallas kernels for 0% -> 0%
where the time goes in v1:
time: 415 us; the launch traced here: 414 us
  waiting for transfers between devices  153 us (37%)
  matrix products  106 us (26%)
  other arithmetic  73.8 us (18%)
  local copies, waits for them, and re-layouts  38 us (9%)
  starting transfers between devices  28.1 us (7%)
  blocking collectives  12.8 us (3%)
    all_to_all x4, waiting for transfers between devices, exchange_in_order(): out = lax.all_to_all(out, axes[k], k, k, tiled=True)  114 us
    dot_general x6, matrix products, one_block(): jnp.einsum('nhqk,nkhd->nqhd', weights, value_rows, preferred_element_type...  68.4 us
    sub x6, other arithmetic, one_block(): weights = jax.nn.softmax(scores, axis=-1).astype(jnp.bfloat16)  67.1 us
    dot_general x6, matrix products, one_block(): jnp.einsum('nqhd,nkhd->nhqk', query_part, key_rows, preferred_element_typ...  38 us
    unnamed x42, local copies, waits for them, and re-layouts  24.8 us
    all_to_all x4, starting transfers between devices, exchange_in_order(): out = lax.all_to_all(out, axes[k], k, k, tiled=True)  22.4 us
    all_to_all x1, waiting for transfers between devices, produce_patches(): jax.lax.all_to_all(jnp.stack(jnp.split(u, jax.lax.axis_size(chip_axis), a...  22.2 us
    ppermute x1, waiting for transfers between devices, from_partner(): return lax.ppermute(block, axis, route)  16.3 us
  transfers between devices with their start and end apart: 6, of which 6 were waited for; matrix products, arithmetic and copies ran while one was open for 3% of the time, Pallas kernels for 0%

profile of v1, /device:TPU:6, one launch (start us, length us, event | category | flops | bytes accessed | tf_op | source)
XLA Modules:
  0.0 414.1 jit_solution(17357988313977811335)
XLA Ops:
  0.6 1.7 copy.97
  2.4 1.8 copy.76
  4.1 11.3 %all-to-all-start.2 = ((bf16[16,2,2,96,128]{4,3,1,2,0:T(8,128)(2,1)}), bf16[16,2,2,96,128]{4,3,1,2,0:T(8,128)(2,1)S(1)}, u32[]{:S(2)}, u32[]{:S(2)}) async-start(bf16[16,2,2,96,128]{4,3,1,2,0:T(8,128)(2,1)} %copy.76), calls=%async_computation.2 | async-start | bytes 3145728 | tf_op jit(solution)/shard_map/all_to_all | solution.py:30
  15.8 1.8 copy.81
  17.6 39.5 %all-to-all-done.2 = bf16[16,2,2,96,128]{4,3,1,2,0:T(8,128)(2,1)S(1)} async-done(((bf16[16,2,2,96,128]{4,3,1,2,0:T(8,128)(2,1)}), bf16[16,2,2,96,128]{4,3,1,2,0:T(8,128)(2,1)S(1)}, u32[]{:S(2)}, u32[]{:S(2)}) %all-to-all-start.2) | async-done | bytes 1572896 | tf_op jit(solution)/shard_map/all_to_all | solution.py:30
  57.1 3.7 all-to-all-start.4
  60.8 1.7 copy.96
  62.6 1.8 copy.72
  64.3 1.3 copy.77
  65.6 35.8 %all-to-all-done.4 = bf16[16,2,2,96,128]{4,3,1,2,0:T(8,128)(2,1)S(1)} async-done(((bf16[16,2,2,96,128]{4,3,1,2,0:T(8,128)(2,1)}), bf16[16,2,2,96,128]{4,3,1,2,0:T(8,128)(2,1)S(1)}, u32[]{:S(2)}, u32[]{:S(2)}) %all-to-all-start.4) | async-done | bytes 1572896 | tf_op jit(solution)/shard_map/all_to_all | solution.py:30
  101.5 3.7 all-to-all-start.3
  105.2 1.3 copy.82
  106.5 1.2 all-to-all-done.3
  107.6 7.8 %all_to_all.35 = bf16[16,2,2,96,128]{4,3,0,2,1:T(8,128)(2,1)} all-to-all(bf16[16,2,2,96,128]{4,3,0,2,1:T(8,128)(2,1)} %copy.82), channel_id=1, replica_groups=mesh['expert'=2,'batch'=4,'seq_0'=4,'seq_1'=4,'seq_2'=2] {'seq_2'}, dimensions={1} | all-to-all | bytes 3145728 | tf_op jit(solution)/shard_map/all_to_all | solution.py:30
  115.5 3.7 all-to-all-start
  119.5 1.3 copy-done
  121.0 1.3 copy.84
  122.3 37.7 %all-to-all-done = bf16[16,2,2,96,128]{4,3,1,2,0:T(8,128)(2,1)S(1)} async-done(((bf16[16,2,2,96,128]{4,3,1,2,0:T(8,128)(2,1)}), bf16[16,2,2,96,128]{4,3,1,2,0:T(8,128)(2,1)S(1)}, u32[]{:S(2)}, u32[]{:S(2)}) %all-to-all-start) | async-done | bytes 1572896 | tf_op jit(solution)/shard_map/all_to_all | solution.py:30
  160.1 5.0 %all_to_all.36 = bf16[16,2,2,96,128]{4,3,0,2,1:T(8,128)(2,1)S(1)} all-to-all(bf16[16,2,2,96,128]{4,3,0,2,1:T(8,128)(2,1)S(1)} %copy.73), channel_id=1, replica_groups=mesh['expert'=2,'batch'=4,'seq_0'=4,'seq_1'=4,'seq_2'=2] {'seq_2'}, dimensions={1} | all-to-all | bytes 3145728 | tf_op jit(solution)/shard_map/all_to_all | solution.py:30
  165.2 173.5 %while.10 = (s32[]{:T(128)}, bf16[6,2,512,1,128]{4,2,1,3,0:T(8,128)(2,1)}, bf16[6,2,512,1,128]{4,2,0,1,3:T(8,128)(2,1)S(1)}, bf16[2,3072,1,128]{3,1,0,2:T(8,128)...) while((s32[]{:T(128)}, bf16[6,2,512,1,128]{4,2,1,3,0:T(8,128)(2,1)}, ...), condition=%wide.region_3.4_spmd, body=%wide.region_0.3_spmd.sunk | while | flops 1639062528 | bytes 54010440 | solution.py:80
  165.2 6.3 %fusion.50 = f32[2,512,3072]{2,1,0:T(8,128)} fusion(bf16[2,3072,1,128]{3,1,0,2:T(8,128)(2,1)S(1)} %get-tuple-element.115, bf16[6,2,512,1,128]{4,2,0,1,3:T(8,128)(2,1)S(1)} %get-tuple-element.114, s32[]{:T(128)} %get-tuple-element.106), kind=kOutput, calls=%fused_computation.8.clone.1 | convolution fusion | flops 805306368 | bytes 14417924 | tf_op jit(solution)/shard_map/while/body/eval_jaxpr/nqhd,nkhd->nhqk/dot_general | solution.py:72
  171.6 11.2 %fusion.51 = f32[2,512]{1,0:T(2,128)S(1)} fusion(f32[2,512,3072]{2,1,0:T(8,128)} %fusion.50), kind=kOutput, calls=%fused_computation.101.clone.1 | output fusion | flops 12585983 | bytes 12587008 | tf_op jit(solution)/shard_map/while/body/eval_jaxpr/sub | solution.py:75
  182.8 11.4 %fusion.52 = bf16[6,2,512,1,128]{4,2,1,3,0:T(8,128)(2,1)} fusion(bf16[6,2,512,1,128]{4,2,1,3,0:T(8,128)(2,1)} %get-tuple-element.107, s32[]{:T(128)} %get-tuple-element.106, bf16[2,3072,1,128]{3,1,0,2:T(8,128)(2,1)} %get-tuple-element.116, f32[2,512]{1,0:T(2,128)S(1)} %fusion.51, f32[2,512,3072]{2,1,0:T(8,128)} %fusion.50), kind=kOutput, calls=%fused_computation.12.clone.1 | convolution fusion | flops 821170176 | bytes 27005440 | tf_op jit(solution)/shard_map/while/body/eval_jaxpr/nhqk,nkhd->nqhd/dot_general | solution.py:76
  194.2 6.3 %fusion.50 = f32[2,512,3072]{2,1,0:T(8,128)} fusion(bf16[2,3072,1,128]{3,1,0,2:T(8,128)(2,1)S(1)} %get-tuple-element.115, bf16[6,2,512,1,128]{4,2,0,1,3:T(8,128)(2,1)S(1)} %get-tuple-element.114, s32[]{:T(128)} %get-tuple-element.106), kind=kOutput, calls=%fused_computation.8.clone.1 | convolution fusion | flops 805306368 | bytes 14417924 | tf_op jit(solution)/shard_map/while/body/eval_jaxpr/nqhd,nkhd->nhqk/dot_general | solution.py:72
  200.5 11.2 %fusion.51 = f32[2,512]{1,0:T(2,128)S(1)} fusion(f32[2,512,3072]{2,1,0:T(8,128)} %fusion.50), kind=kOutput, calls=%fused_computation.101.clone.1 | output fusion | flops 12585983 | bytes 12587008 | tf_op jit(solution)/shard_map/while/body/eval_jaxpr/sub | solution.py:75
  211.7 11.4 %fusion.52 = bf16[6,2,512,1,128]{4,2,1,3,0:T(8,128)(2,1)} fusion(bf16[6,2,512,1,128]{4,2,1,3,0:T(8,128)(2,1)} %get-tuple-element.107, s32[]{:T(128)} %get-tuple-element.106, bf16[2,3072,1,128]{3,1,0,2:T(8,128)(2,1)} %get-tuple-element.116, f32[2,512]{1,0:T(2,128)S(1)} %fusion.51, f32[2,512,3072]{2,1,0:T(8,128)} %fusion.50), kind=kOutput, calls=%fused_computation.12.clone.1 | convolution fusion | flops 821170176 | bytes 27005440 | tf_op jit(solution)/shard_map/while/body/eval_jaxpr/nhqk,nkhd->nqhd/dot_general | solution.py:76
  223.1 6.3 %fusion.50 = f32[2,512,3072]{2,1,0:T(8,128)} fusion(bf16[2,3072,1,128]{3,1,0,2:T(8,128)(2,1)S(1)} %get-tuple-element.115, bf16[6,2,512,1,128]{4,2,0,1,3:T(8,128)(2,1)S(1)} %get-tuple-element.114, s32[]{:T(128)} %get-tuple-element.106), kind=kOutput, calls=%fused_computation.8.clone.1 | convolution fusion | flops 805306368 | bytes 14417924 | tf_op jit(solution)/shard_map/while/body/eval_jaxpr/nqhd,nkhd->nhqk/dot_general | solution.py:72
  229.4 11.2 %fusion.51 = f32[2,512]{1,0:T(2,128)S(1)} fusion(f32[2,512,3072]{2,1,0:T(8,128)} %fusion.50), kind=kOutput, calls=%fused_computation.101.clone.1 | output fusion | flops 12585983 | bytes 12587008 | tf_op jit(solution)/shard_map/while/body/eval_jaxpr/sub | solution.py:75
  240.6 11.4 %fusion.52 = bf16[6,2,512,1,128]{4,2,1,3,0:T(8,128)(2,1)} fusion(bf16[6,2,512,1,128]{4,2,1,3,0:T(8,128)(2,1)} %get-tuple-element.107, s32[]{:T(128)} %get-tuple-element.106, bf16[2,3072,1,128]{3,1,0,2:T(8,128)(2,1)} %get-tuple-element.116, f32[2,512]{1,0:T(2,128)S(1)} %fusion.51, f32[2,512,3072]{2,1,0:T(8,128)} %fusion.50), kind=kOutput, calls=%fused_computation.12.clone.1 | convolution fusion | flops 821170176 | bytes 27005440 | tf_op jit(solution)/shard_map/while/body/eval_jaxpr/nhqk,nkhd->nqhd/dot_general | solution.py:76
  252.0 6.3 %fusion.50 = f32[2,512,3072]{2,1,0:T(8,128)} fusion(bf16[2,3072,1,128]{3,1,0,2:T(8,128)(2,1)S(1)} %get-tuple-element.115, bf16[6,2,512,1,128]{4,2,0,1,3:T(8,128)(2,1)S(1)} %get-tuple-element.114, s32[]{:T(128)} %get-tuple-element.106), kind=kOutput, calls=%fused_computation.8.clone.1 | convolution fusion | flops 805306368 | bytes 14417924 | tf_op jit(solution)/shard_map/while/body/eval_jaxpr/nqhd,nkhd->nhqk/dot_general | solution.py:72
  258.3 11.2 %fusion.51 = f32[2,512]{1,0:T(2,128)S(1)} fusion(f32[2,512,3072]{2,1,0:T(8,128)} %fusion.50), kind=kOutput, calls=%fused_computation.101.clone.1 | output fusion | flops 12585983 | bytes 12587008 | tf_op jit(solution)/shard_map/while/body/eval_jaxpr/sub | solution.py:75
  269.5 11.4 %fusion.52 = bf16[6,2,512,1,128]{4,2,1,3,0:T(8,128)(2,1)} fusion(bf16[6,2,512,1,128]{4,2,1,3,0:T(8,128)(2,1)} %get-tuple-element.107, s32[]{:T(128)} %get-tuple-element.106, bf16[2,3072,1,128]{3,1,0,2:T(8,128)(2,1)} %get-tuple-element.116, f32[2,512]{1,0:T(2,128)S(1)} %fusion.51, f32[2,512,3072]{2,1,0:T(8,128)} %fusion.50), kind=kOutput, calls=%fused_computation.12.clone.1 | convolution fusion | flops 821170176 | bytes 27005440 | tf_op jit(solution)/shard_map/while/body/eval_jaxpr/nhqk,nkhd->nqhd/dot_general | solution.py:76
  280.9 6.3 %fusion.50 = f32[2,512,3072]{2,1,0:T(8,128)} fusion(bf16[2,3072,1,128]{3,1,0,2:T(8,128)(2,1)S(1)} %get-tuple-element.115, bf16[6,2,512,1,128]{4,2,0,1,3:T(8,128)(2,1)S(1)} %get-tuple-element.114, s32[]{:T(128)} %get-tuple-element.106), kind=kOutput, calls=%fused_computation.8.clone.1 | convolution fusion | flops 805306368 | bytes 14417924 | tf_op jit(solution)/shard_map/while/body/eval_jaxpr/nqhd,nkhd->nhqk/dot_general | solution.py:72
  287.3 11.2 %fusion.51 = f32[2,512]{1,0:T(2,128)S(1)} fusion(f32[2,512,3072]{2,1,0:T(8,128)} %fusion.50), kind=kOutput, calls=%fused_computation.101.clone.1 | output fusion | flops 12585983 | bytes 12587008 | tf_op jit(solution)/shard_map/while/body/eval_jaxpr/sub | solution.py:75
  298.4 11.4 %fusion.52 = bf16[6,2,512,1,128]{4,2,1,3,0:T(8,128)(2,1)} fusion(bf16[6,2,512,1,128]{4,2,1,3,0:T(8,128)(2,1)} %get-tuple-element.107, s32[]{:T(128)} %get-tuple-element.106, bf16[2,3072,1,128]{3,1,0,2:T(8,128)(2,1)} %get-tuple-element.116, f32[2,512]{1,0:T(2,128)S(1)} %fusion.51, f32[2,512,3072]{2,1,0:T(8,128)} %fusion.50), kind=kOutput, calls=%fused_computation.12.clone.1 | convolution fusion | flops 821170176 | bytes 27005440 | tf_op jit(solution)/shard_map/while/body/eval_jaxpr/nhqk,nkhd->nqhd/dot_general | solution.py:76
  309.8 6.3 %fusion.50 = f32[2,512,3072]{2,1,0:T(8,128)} fusion(bf16[2,3072,1,128]{3,1,0,2:T(8,128)(2,1)S(1)} %get-tuple-element.115, bf16[6,2,512,1,128]{4,2,0,1,3:T(8,128)(2,1)S(1)} %get-tuple-element.114, s32[]{:T(128)} %get-tuple-element.106), kind=kOutput, calls=%fused_computation.8.clone.1 | convolution fusion | flops 805306368 | bytes 14417924 | tf_op jit(solution)/shard_map/while/body/eval_jaxpr/nqhd,nkhd->nhqk/dot_general | solution.py:72
  316.2 11.2 %fusion.51 = f32[2,512]{1,0:T(2,128)S(1)} fusion(f32[2,512,3072]{2,1,0:T(8,128)} %fusion.50), kind=kOutput, calls=%fused_computation.101.clone.1 | output fusion | flops 12585983 | bytes 12587008 | tf_op jit(solution)/shard_map/while/body/eval_jaxpr/sub | solution.py:75
  327.4 11.4 %fusion.52 = bf16[6,2,512,1,128]{4,2,1,3,0:T(8,128)(2,1)} fusion(bf16[6,2,512,1,128]{4,2,1,3,0:T(8,128)(2,1)} %get-tuple-element.107, s32[]{:T(128)} %get-tuple-element.106, bf16[2,3072,1,128]{3,1,0,2:T(8,128)(2,1)} %get-tuple-element.116, f32[2,512]{1,0:T(2,128)S(1)} %fusion.51, f32[2,512,3072]{2,1,0:T(8,128)} %fusion.50), kind=kOutput, calls=%fused_computation.12.clone.1 | convolution fusion | flops 821170176 | bytes 27005440 | tf_op jit(solution)/shard_map/while/body/eval_jaxpr/nhqk,nkhd->nqhd/dot_general | solution.py:76
  338.8 1.5 fusion.38
  340.7 0.6 constant_dynamic-update-slice_fusion.31
  341.3 0.6 constant_dynamic-update-slice_fusion.30
  341.9 0.6 constant_dynamic-update-slice_fusion.29
  342.5 0.6 constant_dynamic-update-slice_fusion.28
  343.1 0.6 constant_dynamic-update-slice_fusion.27
  343.7 0.6 constant_dynamic-update-slice_fusion.26
  344.3 0.6 constant_dynamic-update-slice_fusion.25
  344.9 0.6 constant_dynamic-update-slice_fusion.24
  345.5 0.6 constant_dynamic-update-slice_fusion.23
  346.2 0.6 constant_dynamic-update-slice_fusion.22
  346.8 0.6 constant_dynamic-update-slice_fusion.21
  347.4 0.6 constant_dynamic-update-slice_fusion.20
  348.0 0.6 constant_dynamic-update-slice_fusion.19
  348.6 0.6 constant_dynamic-update-slice_fusion.18
  349.2 0.6 constant_dynamic-update-slice_fusion.17
  349.8 0.6 constant_dynamic-update-slice_fusion.16
  350.4 0.6 constant_dynamic-update-slice_fusion.15
  360.2 5.7 %all-to-all-start.6 = ((bf16[32,96,128]{2,1,0:T(8,128)(2,1)}), bf16[32,96,128]{2,1,0:T(8,128)(2,1)S(1)}, u32[]{:S(2)}, u32[]{:S(2)}) async-start(bf16[32,96,128]{2,1,0:T(8,128)(2,1)} %constant_dynamic-update-slice_fusion), calls=%async_computation.6 | async-start | bytes 1572864 | tf_op jit(solution)/shard_map/all_to_all | solution.py:95
  367.3 22.2 %all-to-all-done.6 = bf16[32,96,128]{2,1,0:T(8,128)(2,1)S(1)} async-done(((bf16[32,96,128]{2,1,0:T(8,128)(2,1)}), bf16[32,96,128]{2,1,0:T(8,128)(2,1)S(1)}, u32[]{:S(2)}, u32[]{:S(2)}) %all-to-all-start.6) | async-done | bytes 786464 | tf_op jit(solution)/shard_map/all_to_all | solution.py:95
  390.1 0.8 copy-done.1
  390.9 1.2 fusion.31
  392.1 0.9 copy.86
  393.3 2.4 fusion.29
  395.7 16.3 %collective-permute-done = bf16[96,4096]{1,0:T(8,128)(2,1)} collective-permute-done((bf16[96,4096]{1,0:T(8,128)(2,1)}, bf16[96,4096]{1,0:T(8,128)(2,1)}, u32[]{:S(2)}, u32[]{:S(2)}) %collective-permute-start) | collective-permute-done | bytes 786464 | tf_op jit(solution)/shard_map/ppermute | solution.py:47
  412.0 2.1 select_bitcast_fusion
  (35 shorter events, 11.6 us)
Async XLA Ops:
  4.1 11.3 %copy-start.2 = (bf16[1,1,2,96,4096]{4,3,2,1,0:T(8,128)(2,1)S(1)}, bf16[1,1,2,96,4096]{4,3,2,1,0:T(8,128)(2,1)}, u32[]{:S(2)}) copy-start(bf16[1,1,2,96,4096]{4,3,2,1,0:T(8,128)(2,1)} %param.11) | copy-start | bytes 4718596
  4.1 53.0 %all-to-all-start.2 = ((bf16[16,2,2,96,128]{4,3,1,2,0:T(8,128)(2,1)}), bf16[16,2,2,96,128]{4,3,1,2,0:T(8,128)(2,1)S(1)}, u32[]{:S(2)}, u32[]{:S(2)}) async-start(bf16[16,2,2,96,128]{4,3,1,2,0:T(8,128)(2,1)} %copy.76), calls=%async_computation.2 | async-start | bytes 3145728 | tf_op jit(solution)/shard_map/all_to_all | solution.py:30
  57.1 44.4 %all-to-all-start.4 = ((bf16[16,2,2,96,128]{4,3,1,2,0:T(8,128)(2,1)}), bf16[16,2,2,96,128]{4,3,1,2,0:T(8,128)(2,1)S(1)}, u32[]{:S(2)}, u32[]{:S(2)}) async-start(bf16[16,2,2,96,128]{4,3,1,2,0:T(8,128)(2,1)} %copy.81), calls=%async_computation.4 | async-start | bytes 3145728 | tf_op jit(solution)/shard_map/all_to_all | solution.py:30
  101.5 6.2 %all-to-all-start.3 = ((bf16[16,2,2,96,128]{4,3,0,2,1:T(8,128)(2,1)}), bf16[16,2,2,96,128]{4,3,0,2,1:T(8,128)(2,1)S(1)}, u32[]{:S(2)}, u32[]{:S(2)}) async-start(bf16[16,2,2,96,128]{4,3,0,2,1:T(8,128)(2,1)} %copy.77), calls=%async_computation.3 | async-start | bytes 3145728 | tf_op jit(solution)/shard_map/all_to_all | solution.py:30
  115.5 44.5 %all-to-all-start = ((bf16[16,2,2,96,128]{4,3,1,2,0:T(8,128)(2,1)}), bf16[16,2,2,96,128]{4,3,1,2,0:T(8,128)(2,1)S(1)}, u32[]{:S(2)}, u32[]{:S(2)}) async-start(bf16[16,2,2,96,128]{4,3,1,2,0:T(8,128)(2,1)} %copy.72), calls=%async_computation | async-start | bytes 3145728 | tf_op jit(solution)/shard_map/all_to_all | solution.py:30
  119.4 1.4 copy-start
  341.3 25.2 %copy-start.3 = (bf16[1,4096]{1,0:T(2,128)(2,1)S(1)}, bf16[1,4096]{1,0:T(2,128)(2,1)}, u32[]{:S(2)}) copy-start(bf16[1,4096]{1,0:T(2,128)(2,1)} %param.13) | copy-start | bytes 24580
  360.2 29.3 %all-to-all-start.6 = ((bf16[32,96,128]{2,1,0:T(8,128)(2,1)}), bf16[32,96,128]{2,1,0:T(8,128)(2,1)S(1)}, u32[]{:S(2)}, u32[]{:S(2)}) async-start(bf16[32,96,128]{2,1,0:T(8,128)(2,1)} %constant_dynamic-update-slice_fusion), calls=%async_computation.6 | async-start | bytes 1572864 | tf_op jit(solution)/shard_map/all_to_all | solution.py:95
  389.7 1.1 copy-start.1
  392.1 19.9 %collective-permute-start = (bf16[96,4096]{1,0:T(8,128)(2,1)}, bf16[96,4096]{1,0:T(8,128)(2,1)}, u32[]{:S(2)}, u32[]{:S(2)}) collective-permute-start(bf16[96,4096]{1,0:T(8,128)(2,1)} %fusion.31), channel_id=1, source_target_pairs={{0,128},{128,0},{1,129},{129,1},{2,130},{130,2},{3,131},{131,3},{4... | collective-permute-start | bytes 2359304 | tf_op jit(solution)/shard_map/ppermute | solution.py:47
